TPU v7x, 128 devices: a whole 4x4x4 slice. The times are simulated.
128 devices in a mesh: row: 8 (over z, x_hi), col: 16 (over x_lo, y, core).
Axes of the slice: x: 4 (x_hi: 2, x_lo: 2; x = x_hi * 2 + x_lo), y: 4, z: 4, core: 2. Of those that a mesh axis runs over, the one named last changes fastest.
Arguments:
- downdates: float32 [16384, 16384], P('row', 'col'), may hold values from -4 to 4
- centers: float32 [440, 16384], P(None, ('row', 'col')), may hold values from -6 to 6
- diag_inverse: float32 [1024, 1024], P('col'), as said below
- block_map: int32 [16], replicated, may hold values from 0 to 15, each once
- panel_index: int32 [1], replicated, may hold values from 0 to 7
Outputs:
- panel_factor: float32 [16384, 1024], P(('row', 'col'))
- remaining: float32 [16384, 16384], P('row', 'col')
Inputs may be any that keep to these rules, and one draw needn't show every extreme that they name: diag_inverse is lower triangular with a positive diagonal.
All inputs are finite; a program needn't handle non-finite values.
Results may differ from a plain program's by a relative error of at most 0.0003.
Values sent between devices are 32-bit elements; how exact they have to be, the bound alone decides.
A program may use at most 128 MiB of HBM per device.

v0:
```python
import jax
import jax.numpy as jnp
from jax import lax
from jax.sharding import PartitionSpec as P

PANEL = 1024
FEAT = 440
BLOCKS = 16


highest = lax.Precision.HIGHEST


def broadcast(value, axis, source):
    kept = jnp.where(lax.axis_index(axis) == source, value, 0).astype(value.dtype)
    return lax.psum(kept, axis)


def kernel_tile(left_side, right_side):
    left_norm = jnp.sum(left_side * left_side, axis=0)
    right_norm = jnp.sum(right_side * right_side, axis=0)
    cross_term = lax.dot_general(
        left_side,
        right_side,
        (((0,), (0,)), ((), ())),
        precision=highest,
        preferred_element_type=jnp.float32,
    )
    return jnp.exp(-(0.5 / FEAT) * (left_norm[:, None] + right_norm[None, :] - 2.0 * cross_term))


def triangular_apply(row_block, inverse, alive_rows):
    product = lax.dot_general(
        row_block,
        inverse,
        (((1,), (1,)), ((), ())),
        precision=highest,
        preferred_element_type=jnp.float32,
    )
    return jnp.where(alive_rows[:, None], product, 0.0)


def shards(downdates, centers, diag_inverse, block_map, panel_index):
    rows_dev = downdates.shape[0]
    cols_dev = downdates.shape[1]
    col_count = lax.axis_size("col")
    col_pos = lax.axis_index("col")
    row_pos = lax.axis_index("row")
    row_centers, inverse = (
        lax.all_gather(centers, "col", axis=1, tiled=True),
        lax.all_gather(diag_inverse, "col", axis=0, tiled=True),
    )
    source_row = col_pos * cols_dev // rows_dev
    side_start = col_pos * cols_dev - source_row * rows_dev
    col_send = lax.dynamic_slice_in_dim(row_centers, side_start, cols_dev, 1)
    col_centers = broadcast(col_send, "row", source_row)
    assembled = kernel_tile(row_centers, col_centers) + downdates
    panel_number = panel_index[0]
    block_ids = jnp.arange(BLOCKS, dtype=jnp.int32)
    panel_block = jnp.sum(block_ids * (block_map == panel_number).astype(jnp.int32))
    owner_col = panel_block * PANEL // cols_dev
    global_rows = row_pos * rows_dev + jnp.arange(rows_dev, dtype=jnp.int32)
    block_table = (global_rows // PANEL)[:, None] == block_ids[None, :]
    row_alive = jnp.sum(jnp.where(block_table, block_map[None, :], 0), axis=1) > panel_number
    share_rows = rows_dev // col_count
    local_factor = triangular_apply(assembled, inverse, row_alive)
    factor_rows = broadcast(local_factor, "col", owner_col)
    factor_piece = lax.dynamic_slice_in_dim(factor_rows, col_pos * share_rows, share_rows, 0)
    side_send = lax.dynamic_slice_in_dim(factor_rows, side_start, cols_dev, 0)
    factor_cols = broadcast(side_send, "row", source_row)
    update = lax.dot_general(
        factor_rows,
        factor_cols,
        (((1,), (1,)), ((), ())),
        precision=highest,
        preferred_element_type=jnp.float32,
    )
    remaining = assembled - update
    return (factor_piece, remaining)


def solution(mesh):
    return jax.shard_map(
        shards,
        mesh=mesh,
        in_specs=(P("row", "col"), P(None, ("row", "col")), P("col", None), P(), P()),
        out_specs=(P(("row", "col"), None), P("row", "col")),
        check_vma=False,
    )
```

profile of v0, /device:TPU:40, one launch (start us, length us, event | category | flops | bytes accessed | tf_op | source)
XLA Modules:
  0.0 634.6 jit_solution(1171366351438761828)
XLA Ops:
  7.2 0.0 all-gather.3.cloned.1.call-start
  7.2 0.7 all-gather.3.cloned.1.call-update
  7.9 0.0 all-reduce.4.cloned.1.call-start
  8.0 46.1 %all-gather.3.cloned.1.call-done = f32[440,2048]{1,0:T(8,128)} async-done(((f32[440,128]{1,0:T(8,128)}), f32[440,2048]{1,0:T(8,128)}) %all-gather.3.cloned.1.call-update) | async-done | bytes 3604496 | tf_op jit(solution)/shard_map/all_gather | solution.py:50
  54.0 2.9 dynamic-slice_select_fusion.1
  57.0 0.0 all-reduce.4.cloned.1.call-update
  57.0 0.0 all-gather.5.cloned.1.call-start
  57.0 0.7 all-gather.5.cloned.1.call-update
  57.7 0.0 all-reduce.6.cloned.1.call-start
  58.4 1.3 fusion.6
  60.4 0.0 copy-start
  60.4 9.2 %copy.10 = f32[2048,1024]{0,1:T(8,128)} copy(f32[2048,1024]{1,0:T(8,128)} %param.5) | data formatting | bytes 16777216 | tf_op args[0]
  69.6 0.0 copy-done
  69.6 0.1 select_reduce_fusion
  69.7 2.3 multiply_reduce_fusion
  72.0 85.1 %all-reduce.4.cloned.1.call-done = f32[440,1024]{1,0:T(8,128)} async-done(((f32[440,1024]{1,0:T(8,128)}), f32[440,1024]{1,0:T(8,128)}) %all-reduce.4.cloned.1.call-update) | async-done | bytes 1802256 | tf_op jit(solution)/shard_map/psum | solution.py:16
  157.1 1.6 multiply_reduce_fusion.1
  158.7 19.7 %fusion.2 = f32[2048,1024]{0,1:T(8,128)} fusion(f32[2048,1024]{0,1:T(8,128)} %copy.10, f32[440,1024]{1,0:T(8,128)} %all-reduce.4.cloned.1.call-done, f32[440,2048]{1,0:T(8,128)} %all-gather.3.cloned.1.call-done, f32[1024]{0:T(1024)S(1)} %multiply_reduce_fusion.1, f32[2048]{0:T(1024)S(1)} %multiply_reduce_fusion), kind=kOutput, calls=%fused_computation.3 | convolution fusion | flops 11083448320 | bytes 22196224 | tf_op jit(solution)/shard_map/dot_general | solution.py:22
  178.4 18.1 %all-gather.5.cloned.1.call-done = f32[1024,1024]{1,0:T(8,128)} async-done(((f32[64,1024]{1,0:T(8,128)}), f32[1024,1024]{1,0:T(8,128)}) %all-gather.5.cloned.1.call-update) | async-done | bytes 4194320 | tf_op jit(solution)/shard_map/all_gather | solution.py:51
  196.5 57.8 %select_select_fusion = f32[2048,1024]{1,0:T(8,128)} fusion(pred[2048]{0:T(1024)(128)(4,1)S(1)} %broadcast_compare_fusion, pred[]{:T(512)S(6)} %eq.28, f32[2048,1024]{0,1:T(8,128)} %fusion.2, f32[1024,1024]{1,0:T(8,128)} %all-gather.5.cloned.1.call-done), kind=kOutput, calls=%fused_computation.4 | convolution fusion | flops 25773998080 | bytes 20973568 | tf_op jit(solution)/shard_map/dot_general | solution.py:33
  254.4 0.0 all-reduce.6.cloned.1.call-update
  254.4 0.0 all-reduce.8.cloned.1.call-start
  254.4 139.5 %all-reduce.6.cloned.1.call-done = f32[2048,1024]{1,0:T(8,128)} async-done(((f32[2048,1024]{1,0:T(8,128)}), f32[2048,1024]{1,0:T(8,128)}) %all-reduce.6.cloned.1.call-update) | async-done | bytes 8388624 | tf_op jit(solution)/shard_map/psum | solution.py:16
  394.0 5.0 dynamic-slice_select_fusion
  399.0 0.0 all-reduce.8.cloned.1.call-update
  399.0 1.9 constant_dynamic-slice_fusion
  400.9 186.2 %all-reduce.8.cloned.1.call-done = f32[1024,1024]{1,0:T(8,128)} async-done(((f32[1024,1024]{1,0:T(8,128)}), f32[1024,1024]{1,0:T(8,128)}) %all-reduce.8.cloned.1.call-update) | async-done | bytes 4194320 | tf_op jit(solution)/shard_map/psum | solution.py:16
  587.1 31.7 %convolution_subtract_fusion = f32[2048,1024]{0,1:T(8,128)} fusion(f32[2048,1024]{0,1:T(8,128)} %fusion.2, f32[2048,1024]{1,0:T(8,128)} %all-reduce.6.cloned.1.call-done, f32[1024,1024]{1,0:T(8,128)} %all-reduce.8.cloned.1.call-done), kind=kOutput, calls=%fused_computation.6 | convolution fusion | flops 25771900928 | bytes 29360128 | tf_op jit(solution)/shard_map/dot_general | solution.py:71
  618.8 9.2 %copy.12 = f32[2048,1024]{1,0:T(8,128)} copy(f32[2048,1024]{0,1:T(8,128)} %convolution_subtract_fusion) | data formatting | bytes 16777216
  (2 shorter events, 0.0 us)
Async XLA Ops:
  7.2 46.9 %all-gather.3.cloned.1.call-start = ((), (), s32[]{:S(2)}) async-start(), calls=%async_computation | async-start | bytes 3829760 | tf_op jit(solution)/shard_map/all_gather | solution.py:50
  7.9 149.2 %all-reduce.4.cloned.1.call-start = ((), (), s32[]{:S(2)}) async-start(), calls=%async_computation.1 | async-start | bytes 3604480 | tf_op jit(solution)/shard_map/psum | solution.py:16
  57.0 139.5 %all-gather.5.cloned.1.call-start = ((), (), s32[]{:S(2)}) async-start(), calls=%async_computation.2 | async-start | bytes 4456448 | tf_op jit(solution)/shard_map/all_gather | solution.py:51
  57.7 336.2 %all-reduce.6.cloned.1.call-start = ((), (), s32[]{:S(2)}) async-start(), calls=%async_computation.3 | async-start | bytes 16777216 | tf_op jit(solution)/shard_map/psum | solution.py:16
  60.4 9.2 %copy-start = (s32[16]{0:T(128)S(1)}, s32[16]{0:T(128)}, u32[]{:S(2)}) copy-start(s32[16]{0:T(128)} %param.8) | copy-start | bytes 196
  254.4 332.7 %all-reduce.8.cloned.1.call-start = ((), (), s32[]{:S(2)}) async-start(), calls=%async_computation.4 | async-start | bytes 8388608 | tf_op jit(solution)/shard_map/psum | solution.py:16
Sparse Core Ops, SparseCore 0:
  9.6 44.3 all-gather.2
  57.1 99.9 all-reduce.3
  158.8 37.6 all-gather.4
  254.5 139.4 all-reduce.5
  399.1 187.9 all-reduce.7
where the time goes:
time: 637 us; the launch traced here: 635 us
  waiting for transfers between devices  476 us (75%)
  matrix products  109 us (17%)
  local copies, waits for them, and re-layouts  20.3 us (3%)
  between operations  15.1 us (2%)
  other arithmetic  13.3 us (2%)
    psum x3, waiting for transfers between devices, broadcast(): return lax.psum(kept, axis)  411 us
    dot_general x1, matrix products, triangular_apply(): lax.dot_general(row_block, inverse, (((1,), (1,)), ((), ())), precision=h...  57.8 us
    all_gather x1, waiting for transfers between devices, shards(): lax.all_gather(centers, 'col', axis=1, tiled=True)  46.1 us
    dot_general x1, matrix products, shards(): lax.dot_general(factor_rows, factor_cols, (((1,), (1,)), ((), ())), preci...  31.7 us
    dot_general x1, matrix products, kernel_tile(): lax.dot_general(left_side, right_side, (((0,), (0,)), ((), ())), precisio...  19.7 us
    unnamed x4, local copies, waits for them, and re-layouts  18.4 us
    all_gather x1, waiting for transfers between devices, shards(): lax.all_gather(diag_inverse, 'col', axis=0, tiled=True)  18.1 us
  transfers between devices with their start and end apart: 5, of which 5 were waited for; matrix products, arithmetic and copies ran while one was open for 6% of the time, Pallas kernels for 0%

commit v1 on v0

v1 whole, which is shorter than its diff:
```python
import functools

import jax
import jax.numpy as jnp
from jax import lax
from jax.experimental import pallas as pl
from jax.experimental.pallas import tpu as pltpu
from jax.sharding import PartitionSpec as P

PANEL = 1024
FEAT = 440
KPAD = 512
BLOCKS = 16
MESH = pl.DeviceIdType.MESH
F32 = jnp.float32
BF16 = jnp.bfloat16
CHUNKS = 16
LAG = 4


def place():
    row = lax.axis_index("row")
    col = lax.axis_index("col")
    return dict(z=row // 2, xh=row % 2, xl=col // 8, y=(col // 2) % 4, a=col % 2)


def device(p, **changes):
    q = dict(p)
    q.update(changes)
    return (q["z"] * 2 + q["xh"], q["xl"] * 8 + q["y"] * 2 + q["a"])


def neighbours(p):
    return dict(
        yp=device(p, y=(p["y"] + 1) % 4),
        ym=device(p, y=(p["y"] + 3) % 4),
        xp=device(p, xl=1 - p["xl"]),
        zp=device(p, z=(p["z"] + 1) % 4),
        zm=device(p, z=(p["z"] + 3) % 4),
        xx=device(p, xh=1 - p["xh"]),
        co=device(p, a=1 - p["a"]),
    )


def entry_barrier(near):
    barrier = pltpu.get_barrier_semaphore()
    for where in near.values():
        pl.semaphore_signal(barrier, inc=1, device_id=where, device_id_type=MESH)
    pl.semaphore_wait(barrier, len(near))


def remote(src, dst, send, recv, where):
    return pltpu.make_async_remote_copy(
        src_ref=src, dst_ref=dst, send_sem=send, recv_sem=recv, device_id=where, device_id_type=MESH
    )


def branch_flags(first_ring, d, m, part):
    rel = (d - m + 16) % 4
    if part == 0:
        up = (first_ring & (d != 3)) | (~first_ring & (rel <= 1))
        down = ~first_ring & (rel == 0)
    else:
        up = ~first_ring & (rel == 0)
        down = (first_ring & (d != 1)) | (~first_ring & ((rel == 0) | (rel == 3)))
    across = first_ring & (rel == 0)
    return up, down, across


def column_state(p):
    k = p["xl"] * 4 + p["y"]
    d = (p["z"] - k // 2 + 4) % 4
    first = p["xh"] == k % 2
    diagonal = (p["z"] * 2 + p["xh"]) == k
    return d, first, diagonal


def gather_kernel(x_ref, l_ref, d_ref, xg, li, dx, own, rx, rl, rk, rc, sx, sl, sk, sc, sd):
    p = place()
    near = neighbours(p)
    a, y, xl = p["a"], p["y"], p["xl"]
    d, first, diagonal = column_state(p)
    entry_barrier(near)

    def slot(xl_, y_, a_):
        return xl_ * 8 + y_ * 2 + a_

    def at(table, s):
        return xg.at[s // 8, s % 8] if table == 0 else li.at[s]

    started = []

    def send(table, s, way, src=None):
        src = at(table, s) if src is None else src
        sems, recv = (sx, rx) if table == 0 else (sl, rl)
        way_index = ("yp", "ym", "xp", "co").index(way)
        copy = remote(src, at(table, s), sems.at[way_index, s], recv.at[s], near[way])
        copy.start()
        started.append(copy)

    def arrived(table, s):
        recv = rx if table == 0 else rl
        copy = pltpu.make_async_copy(at(table, s), at(table, s), recv.at[s])
        copy.wait()

    mine = slot(xl, y, a)
    before, after, far = (y + 3) % 4, (y + 1) % 4, (y + 2) % 4

    def first_sends(table):
        src = x_ref if table == 0 else l_ref
        for way in ("yp", "ym", "xp", "co"):
            send(table, mine, way, src)
        keep = pltpu.make_async_copy(src, at(table, mine), own.at[table])
        keep.start()
        return keep

    keep_x = first_sends(0)
    keep_l = first_sends(1)
    half = PANEL
    swap = remote(d_ref.at[pl.ds((1 - a) * half, half)], dx, sd.at[0], sd.at[1], near["co"])
    swap.start()

    def row_steps(table):
        steps = []

        def step(s, *ways):
            def run():
                arrived(table, s)
                for way in ways:
                    send(table, s, way)

            steps.append(run)

        step(slot(1 - xl, y, a), "yp", "ym", "co")
        if table == 0:
            step(slot(xl, before, a), "yp", "co")
            step(slot(xl, after, a), "co")
        else:
            step(slot(xl, after, a), "ym", "co")
            step(slot(xl, before, a), "co")
        step(slot(1 - xl, before, a), "co")
        step(slot(1 - xl, after, a), "co")
        step(slot(xl, far, a), "xp", "co")
        step(slot(1 - xl, far, a), "co")
        return steps

    for run in row_steps(0):
        run()
    for xs in range(2):
        for ys in range(4):
            arrived(0, slot(xs, ys, 1 - a))
    keep_x.wait()

    def column_copies(m, part, src, is_first, dist):
        up, down, across = branch_flags(is_first, dist, m, part)
        j = 2 * m + part
        dst = xg.at[2 + a, j]
        out = []
        for index, (flag, way) in enumerate(((up, "zp"), (down, "zm"), (across, "xx"))):
            out.append((flag, remote(src, dst, sk.at[index, j], rk.at[j], near[way])))
        return out

    true = d >= 0

    @pl.when(diagonal)
    def _():
        for m in range(4):
            for part in range(2):
                for flag, copy in column_copies(m, part, xg.at[a, 2 * m + part], true, 0 * d):
                    @pl.when(flag)
                    def _():
                        copy.start()

    def column_step(m):
        @pl.when(~diagonal)
        def _():
            for part in range(2):
                j = 2 * m + part
                here = xg.at[2 + a, j]
                pltpu.make_async_copy(here, here, rk.at[j]).wait()
                for flag, copy in column_copies(m, part, here, first, d):
                    @pl.when(flag)
                    def _():
                        copy.start()
                remote(here, here, sc.at[j], rc.at[j], near["co"]).start()

    rest = row_steps(1)
    for run in rest[:3]:
        run()
    column_step(0)
    for run in rest[3:6]:
        run()
    column_step(1)
    rest[6]()
    column_step(2)
    column_step(3)

    for xs in range(2):
        for ys in range(4):
            arrived(1, slot(xs, ys, 1 - a))
    keep_l.wait()
    swap.wait()

    @pl.when(diagonal)
    def _():
        for m in range(4):
            for part in range(2):
                for flag, copy in column_copies(m, part, xg.at[a, 2 * m + part], true, 0 * d):
                    @pl.when(flag)
                    def _():
                        copy.wait_send()

    @pl.when(~diagonal)
    def _():
        for m in range(4):
            for part in range(2):
                j = 2 * m + part
                here = xg.at[2 + a, j]
                for flag, copy in column_copies(m, part, here, first, d):
                    @pl.when(flag)
                    def _():
                        copy.wait_send()
                other = xg.at[3 - a, j]
                remote(here, here, sc.at[j], rc.at[j], near["co"]).wait_send()
                pltpu.make_async_copy(other, other, rc.at[j]).wait()

    for copy in started:
        copy.wait_send()


def gather(centers, inverse, downdates):
    dma = pltpu.SemaphoreType.DMA
    anywhere = pl.BlockSpec(memory_space=pl.ANY)
    vmem = pl.BlockSpec(memory_space=pltpu.VMEM)
    width = centers.shape[1]
    rows = inverse.shape[0]
    return pl.pallas_call(
        gather_kernel,
        out_shape=(
            jax.ShapeDtypeStruct((4, 8, FEAT, width), F32),
            jax.ShapeDtypeStruct((16, rows, PANEL), F32),
            jax.ShapeDtypeStruct((PANEL, PANEL), F32),
        ),
        in_specs=[vmem, vmem, anywhere],
        out_specs=(anywhere, anywhere, anywhere),
        scratch_shapes=[
            dma((2,)),
            dma((16,)),
            dma((16,)),
            dma((8,)),
            dma((8,)),
            dma((4, 16)),
            dma((4, 16)),
            dma((3, 8)),
            dma((8,)),
            dma((2,)),
        ],
        compiler_params=pltpu.CompilerParams(collective_id=0, has_side_effects=True),
        name="gather",
    )(centers, inverse, downdates)


def split(value):
    high = value.astype(BF16)
    low = (value - high.astype(F32)).astype(BF16)
    return high, low


def product(left, right, dims):
    dot = functools.partial(lax.dot_general, dimension_numbers=((dims), ((), ())), preferred_element_type=F32)
    (lh, ll), (rh, rl) = left, right
    return dot(lh, rh) + (dot(lh, rl) + dot(ll, rh))


def set_right(x_ref, high, low, norm):
    width = x_ref.shape[-1]
    for j in range(8):
        block = x_ref[0, j]
        norm[:, j * width : (j + 1) * width] = jnp.sum(block * block, axis=0, keepdims=True)
        block = jnp.concatenate([block, jnp.zeros((KPAD - FEAT, width), F32)], axis=0)
        h, l = split(block)
        high[:, j * width : (j + 1) * width] = h
        low[:, j * width : (j + 1) * width] = l


def gauss_tile(left_ref, high, low, norm):
    left = [left_ref[0, j] for j in range(left_ref.shape[1])]
    width = left[0].shape[1]
    zero = jnp.zeros((KPAD - FEAT, width), F32)
    left = jnp.concatenate([jnp.concatenate([block, zero], axis=0).T for block in left], axis=0)
    left_norm = jnp.sum(left * left, axis=1, keepdims=True)
    cross = product(split(left), (high[...], low[...]), ((1,), (0,)))
    return jnp.exp(-(0.5 / FEAT) * (left_norm + norm[...] - 2.0 * cross))


def factor_kernel(s_ref, xl_ref, xr_ref, li_ref, d_ref, dx_ref, out_ref, high, low, norm, lih, lil):
    @pl.when(pl.program_id(0) == 0)
    def _():
        set_right(xr_ref, high, low, norm)
        h, l = split(li_ref[...])
        lih[...] = h
        lil[...] = l

    raw = gauss_tile(xl_ref, high, low, norm) + jnp.where(s_ref[2] == 1, d_ref[...], dx_ref[...])
    result = product(split(raw), (lih[...], lil[...]), ((1,), (1,)))
    out_ref[...] = jnp.where(s_ref[3] == 1, result, 0.0)


TILE = 256


def panel_factor(scalars, xg, li, downdates, dx):
    per = TILE // xg.shape[-1]
    spec = pltpu.PrefetchScalarGridSpec(
        num_scalar_prefetch=1,
        grid=(PANEL // TILE,),
        in_specs=[
            pl.BlockSpec((1, per, FEAT, xg.shape[-1]), lambda i, s: (s[0], i, 0, 0)),
            pl.BlockSpec((1, 8, FEAT, xg.shape[-1]), lambda i, s: (s[1], 0, 0, 0)),
            pl.BlockSpec((PANEL, PANEL), lambda i, s: (0, 0)),
            pl.BlockSpec((TILE, PANEL), lambda i, s: (s[0] * (PANEL // TILE) + i, 0)),
            pl.BlockSpec((TILE, PANEL), lambda i, s: (i, 0)),
        ],
        out_specs=pl.BlockSpec((TILE, PANEL), lambda i, s: (i, 0)),
        scratch_shapes=[
            pltpu.VMEM((KPAD, PANEL), BF16),
            pltpu.VMEM((KPAD, PANEL), BF16),
            pltpu.VMEM((1, PANEL), F32),
            pltpu.VMEM((PANEL, PANEL), BF16),
            pltpu.VMEM((PANEL, PANEL), BF16),
        ],
    )
    return pl.pallas_call(
        factor_kernel, grid_spec=spec, out_shape=jax.ShapeDtypeStruct((PANEL, PANEL), F32), name="factor"
    )(scalars, xg, xg, li, downdates, dx)


def remaining_kernel(s_ref, xl_ref, xr_ref, fl_ref, fr_ref, piece_ref, d_ref, out_ref, piece_out, high, low, norm, frh, frl):
    @pl.when(pl.program_id(0) == 0)
    def _():
        set_right(xr_ref, high, low, norm)
        h, l = split(fr_ref[0])
        frh[...] = h
        frl[...] = l
        piece_out[...] = piece_ref[0]

    update = product(split(fl_ref[0]), (frh[...], frl[...]), ((1,), (1,)))
    out_ref[...] = gauss_tile(xl_ref, high, low, norm) + d_ref[...] - update


def remaining_matrix(scalars, xg, factors, downdates):
    rows = downdates.shape[0]
    width = xg.shape[-1]
    per = TILE // width
    steps = PANEL // TILE
    spec = pltpu.PrefetchScalarGridSpec(
        num_scalar_prefetch=1,
        grid=(rows // TILE,),
        in_specs=[
            pl.BlockSpec((1, per, FEAT, width), lambda i, s: (i // steps, i % steps, 0, 0)),
            pl.BlockSpec((1, 8, FEAT, width), lambda i, s: (s[4], 0, 0, 0)),
            pl.BlockSpec((1, TILE, PANEL), lambda i, s: (i // steps, i % steps, 0)),
            pl.BlockSpec((1, PANEL, PANEL), lambda i, s: (s[5], 0, 0)),
            pl.BlockSpec((1, width, PANEL), lambda i, s: (s[6], s[7], 0)),
            pl.BlockSpec((TILE, PANEL), lambda i, s: (i, 0)),
        ],
        out_specs=(
            pl.BlockSpec((TILE, PANEL), lambda i, s: (i, 0)),
            pl.BlockSpec((width, PANEL), lambda i, s: (0, 0)),
        ),
        scratch_shapes=[
            pltpu.VMEM((KPAD, PANEL), BF16),
            pltpu.VMEM((KPAD, PANEL), BF16),
            pltpu.VMEM((1, PANEL), F32),
            pltpu.VMEM((PANEL, PANEL), BF16),
            pltpu.VMEM((PANEL, PANEL), BF16),
        ],
    )
    return pl.pallas_call(
        remaining_kernel,
        grid_spec=spec,
        out_shape=(
            jax.ShapeDtypeStruct((rows, PANEL), F32),
            jax.ShapeDtypeStruct((width, PANEL), F32),
        ),
        name="remaining",
    )(scalars, xg, xg, factors, factors, factors, downdates)


def spread_kernel(root, f_ref, g, rrow, rcol, rcore, srow, scol, score):
    p = place()
    near = neighbours(p)
    a = p["a"]
    size = PANEL // (2 * CHUNKS)
    y0, x0 = root % 4, root // 4
    d_row = (p["y"] - y0 + 4) % 4
    first_row = p["xl"] == x0
    is_root = first_row & (d_row == 0)
    d_col, first_col, diagonal = column_state(p)
    true = d_col >= 0
    entry_barrier(near)

    def rows(i):
        return pl.ds(pl.multiple_of(i * size, size), size)

    @pl.when(is_root)
    def _():
        def keep(i, carry):
            pltpu.make_async_copy(f_ref.at[rows(i)], g.at[a, rows(i)], rrow.at[i]).start()
            return carry

        lax.fori_loop(0, 2 * CHUNKS, keep, 0)

    def row_copies(m, part):
        i = m + part * CHUNKS
        here = g.at[a, rows(i)]
        flags = branch_flags(first_row, d_row, m, part)
        out = [
            (flag, remote(here, here, srow.at[n, i], rrow.at[i], near[way]))
            for n, (flag, way) in enumerate(zip(flags, ("yp", "ym", "xp")))
        ]
        out.append((true, remote(here, here, score.at[i], rcore.at[i], near["co"])))
        return out

    def column_copies(m, part, from_row):
        i = m + part * CHUNKS
        src = g.at[a, rows(i)] if from_row else g.at[2, rows(i)]
        dst = g.at[2, rows(i)]
        flags = branch_flags(true, 0 * d_col, m, part) if from_row else branch_flags(first_col, d_col, m, part)
        return [
            (flag, remote(src, dst, scol.at[n, i], rcol.at[i], near[way]))
            for n, (flag, way) in enumerate(zip(flags, ("zp", "zm", "xx")))
        ]

    def each(copies, act):
        for flag, copy in copies:
            @pl.when(flag)
            def _():
                act(copy)

    def row_step(m):
        for part in range(2):
            i = m + part * CHUNKS
            here = g.at[a, rows(i)]
            pltpu.make_async_copy(here, here, rrow.at[i]).wait()
            each(row_copies(m, part), lambda copy: copy.start())

            @pl.when(diagonal)
            def _():
                each(column_copies(m, part, True), lambda copy: copy.start())

    def column_step(m):
        @pl.when(~diagonal)
        def _():
            for part in range(2):
                i = m + part * CHUNKS
                here = g.at[2, rows(i)]
                pltpu.make_async_copy(here, here, rcol.at[i]).wait()
                each(column_copies(m, part, False), lambda copy: copy.start())

    def loop(low, high, body):
        def run(m, carry):
            body(m)
            return carry

        lax.fori_loop(low, high, run, 0)

    loop(0, LAG, row_step)

    def both(m):
        row_step(m)
        column_step(m - LAG)

    loop(LAG, CHUNKS, both)
    loop(CHUNKS - LAG, CHUNKS, column_step)

    def finish(m):
        for part in range(2):
            i = m + part * CHUNKS
            there = g.at[1 - a, rows(i)]
            pltpu.make_async_copy(there, there, rcore.at[i]).wait()
            each(row_copies(m, part), lambda copy: copy.wait_send())

            @pl.when(diagonal)
            def _():
                each(column_copies(m, part, True), lambda copy: copy.wait_send())

            @pl.when(~diagonal)
            def _():
                each(column_copies(m, part, False), lambda copy: copy.wait_send())

    loop(0, CHUNKS, finish)


def spread(root, half):
    dma = pltpu.SemaphoreType.DMA
    n = 2 * CHUNKS
    return pl.pallas_call(
        functools.partial(spread_kernel, root),
        out_shape=jax.ShapeDtypeStruct((3, PANEL, PANEL), F32),
        in_specs=[pl.BlockSpec(memory_space=pltpu.VMEM)],
        out_specs=pl.BlockSpec(memory_space=pl.ANY),
        scratch_shapes=[dma((n,)), dma((n,)), dma((n,)), dma((3, n)), dma((3, n)), dma((n,))],
        compiler_params=pltpu.CompilerParams(collective_id=1 + root, has_side_effects=True),
        name="spread" + str(root),
    )(half)


def shards(downdates, centers, diag_inverse, block_map, panel_index):
    row = lax.axis_index("row")
    col = lax.axis_index("col")
    core = col % 2
    diagonal = row == col // 2
    block_ids = jnp.arange(BLOCKS, dtype=jnp.int32)
    panel_block = jnp.sum(block_ids * (block_map == panel_index[0]).astype(jnp.int32))
    alive = jnp.sum(jnp.where(block_ids == 2 * row + core, block_map, 0)) > panel_index[0]
    base = jnp.where(diagonal, 0, 2)
    scalars = jnp.stack(
        [
            core,
            base + panel_block % 2,
            (panel_block % 2 == core).astype(jnp.int32),
            alive.astype(jnp.int32),
            base + core,
            jnp.where(diagonal, core, 2),
            col // 8,
            col % 8,
        ]
    ).astype(jnp.int32)
    xg, li, dx = gather(centers, diag_inverse, downdates)
    half = panel_factor(scalars, xg, li.reshape(PANEL, PANEL), downdates, dx)
    factors = lax.switch(panel_block // 2, [functools.partial(spread, root) for root in range(BLOCKS // 2)], half)
    remaining, piece = remaining_matrix(scalars, xg, factors, downdates)
    return piece, remaining


def solution(mesh):
    return jax.shard_map(
        shards,
        mesh=mesh,
        in_specs=(P("row", "col"), P(None, ("row", "col")), P("col", None), P(), P()),
        out_specs=(P(("row", "col"), None), P("row", "col")),
        check_vma=False,
    )
```

time: 637 us -> 818 us (1.28)
  Pallas kernels: 0 us -> 802 us
  waiting for transfers between devices: 476 us -> 0 us
  matrix products: 109 us -> 0 us
  local copies, waits for them, and re-layouts: 20.3 us -> 0.64 us
  other arithmetic: 13.3 us -> 1.33 us
  between operations: 15.1 us -> 4.36 us
    pallas_call x0 -> x4, Pallas kernels: none -> 802 us  [the longest x1 610 us: spread(): pl.pallas_call(functools.partial(spread_kernel, root), out_shape=jax.Shap...]
    psum x3 -> x0, waiting for transfers between devices: 411 us -> none  [broadcast(): return lax.psum(kept, axis)]
    dot_general x3 -> x0, matrix products: 109 us -> none  [the longest x1 57.8 us: triangular_apply(): lax.dot_general(row_block, inverse, (((1,), (1,)), ((), ())), precision=h...]
    all_gather x2 -> x0, waiting for transfers between devices: 64.2 us -> none  [the longest x1 46.1 us: shards(): lax.all_gather(centers, 'col', axis=1, tiled=True)]
    unnamed x4 -> x0, local copies, waits for them, and re-layouts: 18.4 us -> none
  transfers between devices with their start and end apart: 5 -> 0, of which waited for: 5 -> 0; matrix products, arithmetic and copies ran while one was open for 6% -> 0% of each run, Pallas kernels for 0% -> 0%
where the time goes in v1:
time: 818 us; the launch traced here: 808 us
  Pallas kernels  802 us (98%)
    pallas_call x1, Pallas kernels, spread(): pl.pallas_call(functools.partial(spread_kernel, root), out_shape=jax.Shap...  610 us
    pallas_call x1, Pallas kernels, gather(): pl.pallas_call(gather_kernel, out_shape=(jax.ShapeDtypeStruct((4, 8, FEAT...  144 us
    pallas_call x1, Pallas kernels, remaining_matrix(): pl.pallas_call(remaining_kernel, grid_spec=spec, out_shape=(jax.ShapeDtyp...  29.8 us
    pallas_call x1, Pallas kernels, panel_factor(): pl.pallas_call(factor_kernel, grid_spec=spec, out_shape=jax.ShapeDtypeStr...  18.4 us

profile of v1, /device:TPU:40, one launch (start us, length us, event | category | flops | bytes accessed | tf_op | source)
XLA Modules:
  0.0 808.5 jit_solution(13514502202079857874)
XLA Ops:
  1.3 1.3 fusion.1
  5.7 0.6 stack.43.s_ref
  6.3 144.0 %gather.1 = (f32[4,8,440,128]{3,2,1,0:T(8,128)}, f32[16,64,1024]{2,1,0:T(8,128)}, f32[1024,1024]{1,0:T(8,128)}) custom-call(f32[440,128]{1,0:T(8,128)} %x_ref.1, f32[64,1024]{1,0:T(8,128)} %l_ref.1, f32[2048,1024]{1,0:T(8,128)} %d_ref.5), custom_call_target="tpu_custom_call" | custom-call | tf_op jit(solution)/shard_map/gather/pallas_call | solution.py:237
  150.3 18.4 %factor.1 = f32[1024,1024]{1,0:T(8,128)} custom-call(s32[8]{0:T(128)} %stack.43.s_ref, f32[4,8,440,128]{3,2,1,0:T(8,128)} %get-tuple-element.24.xl_ref.xr_ref, f32[4,8,440,128]{3,2,1,0:T(8,128)} %get-tuple-element.24.xl_ref.xr_ref, f32[1024,1024]{1,0:T(8,128)} %bitcast.12, f32[2048,1024]{1,0:T(8,128)} %d_ref.5, f32[1024,1024]{1,0:T(8,128)} %get-tuple-element.26.dx_ref), custom_call_target="tpu_custom_call" | custom-call | tf_op jit(solution)/shard_map/factor/pallas_call | solution.py:333
  168.7 610.0 %conditional.1 = (f32[3,1024,1024]{2,1,0:T(8,128)}) conditional(s32[]{:T(128)} %clamp.3, f32[1024,1024]{1,0:T(8,128)} %factor.1, f32[1024,1024]{1,0:T(8,128)} %factor.1, f32[1024,1024]{1,0:T(8,128)} %factor.1, f32[1024,1024]{1,0:T(8,128)} %factor.1, f32[1024,1024]{1,0:T(8,128)} %factor.1, ...), branch_computations={%region_2.3_spmd, %region_3.4_spmd, %region_4.5_spmd, %region_5.6_... | conditional | bytes 8 | solution.py:532
  168.7 609.6 %spread5.1 = f32[3,1024,1024]{2,1,0:T(8,128)} custom-call(f32[1024,1024]{1,0:T(8,128)} %f_ref.5), custom_call_target="tpu_custom_call" | custom-call | tf_op jit(solution)/shard_map/cond/branch_5_fun/spread5/pallas_call | solution.py:498
  778.7 29.8 %remaining.1 = (f32[2048,1024]{1,0:T(8,128)}, f32[128,1024]{1,0:T(8,128)}) custom-call(s32[8]{0:T(128)} %stack.43.s_ref, f32[4,8,440,128]{3,2,1,0:T(8,128)} %get-tuple-element.24.xl_ref.xr_ref, f32[4,8,440,128]{3,2,1,0:T(8,128)} %get-tuple-element.24.xl_ref.xr_ref, f32[3,1024,1024]{2,1,0:T(8,128)} %get-tuple-element.31.fl_ref.fr_ref.piece_ref, ...), custom_call_target="tpu_custom_call" | custom-call | tf_op jit(solution)/shard_map/remaining/pallas_call | solution.py:379

commit v2 on v1

--- a/solution.py
+++ b/solution.py
@@ -14,8 +14,8 @@
 MESH = pl.DeviceIdType.MESH
 F32 = jnp.float32
 BF16 = jnp.bfloat16
-CHUNKS = 16
-LAG = 4
+CHUNKS = 32
+SKEW = 2
 
 
 def place():
@@ -387,6 +387,13 @@
     )(scalars, xg, xg, factors, factors, factors, downdates)
 
 
+def hops(first_ring, d, e, part):
+    rel = (d - e + 4) % 4
+    near_e = e if part == 0 else (4 - e) % 4
+    in_first = d if part == 0 else (4 - d) % 4
+    return jnp.where(first_ring, in_first, near_e + 1 + jnp.minimum(rel, 4 - rel))
+
+
 def spread_kernel(root, f_ref, g, rrow, rcol, rcore, srow, scol, score):
     p = place()
     near = neighbours(p)
@@ -411,10 +418,10 @@
 
         lax.fori_loop(0, 2 * CHUNKS, keep, 0)
 
-    def row_copies(m, part):
+    def row_copies(m, e, part):
         i = m + part * CHUNKS
         here = g.at[a, rows(i)]
-        flags = branch_flags(first_row, d_row, m, part)
+        flags = branch_flags(first_row, d_row, e, part)
         out = [
             (flag, remote(here, here, srow.at[n, i], rrow.at[i], near[way]))
             for n, (flag, way) in enumerate(zip(flags, ("yp", "ym", "xp")))
@@ -422,11 +429,11 @@
         out.append((true, remote(here, here, score.at[i], rcore.at[i], near["co"])))
         return out
 
-    def column_copies(m, part, from_row):
+    def column_copies(m, e, part, from_row):
         i = m + part * CHUNKS
         src = g.at[a, rows(i)] if from_row else g.at[2, rows(i)]
         dst = g.at[2, rows(i)]
-        flags = branch_flags(true, 0 * d_col, m, part) if from_row else branch_flags(first_col, d_col, m, part)
+        flags = branch_flags(true, 0 * d_col, e, part) if from_row else branch_flags(first_col, d_col, e, part)
         return [
             (flag, remote(src, dst, scol.at[n, i], rcol.at[i], near[way]))
             for n, (flag, way) in enumerate(zip(flags, ("zp", "zm", "xx")))
@@ -438,58 +445,62 @@
             def _():
                 act(copy)
 
-    def row_step(m):
+    row_lag = {}
+    col_lag = {}
+    for e in range(4):
         for part in range(2):
-            i = m + part * CHUNKS
-            here = g.at[a, rows(i)]
-            pltpu.make_async_copy(here, here, rrow.at[i]).wait()
-            each(row_copies(m, part), lambda copy: copy.start())
-
-            @pl.when(diagonal)
-            def _():
-                each(column_copies(m, part, True), lambda copy: copy.start())
-
-    def column_step(m):
-        @pl.when(~diagonal)
-        def _():
+            row_lag[e, part] = SKEW * hops(first_row, d_row, e, part)
+            col_lag[e, part] = row_lag[e, part] + SKEW * hops(first_col, d_col, e, part)
+
+    def turn(t, carry):
+        for e in range(4):
+            for part in range(2):
+                m = t - row_lag[e, part]
+
+                @pl.when((m >= 0) & (m < CHUNKS) & ((m + 64) % 4 == e))
+                def _():
+                    i = m + part * CHUNKS
+                    here = g.at[a, rows(i)]
+                    pltpu.make_async_copy(here, here, rrow.at[i]).wait()
+                    each(row_copies(m, e, part), lambda copy: copy.start())
+
+                    @pl.when(diagonal)
+                    def _():
+                        each(column_copies(m, e, part, True), lambda copy: copy.start())
+
+                n = t - col_lag[e, part]
+
+                @pl.when((n >= 0) & (n < CHUNKS) & ((n + 64) % 4 == e) & ~diagonal)
+                def _():
+                    i = n + part * CHUNKS
+                    here = g.at[2, rows(i)]
+                    pltpu.make_async_copy(here, here, rcol.at[i]).wait()
+                    each(column_copies(n, e, part, False), lambda copy: copy.start())
+
+        return carry
+
+    lax.fori_loop(0, CHUNKS + 12 * SKEW, turn, 0)
+
+    def finish(group, carry):
+        for e in range(4):
+            m = group * 4 + e
             for part in range(2):
                 i = m + part * CHUNKS
-                here = g.at[2, rows(i)]
-                pltpu.make_async_copy(here, here, rcol.at[i]).wait()
-                each(column_copies(m, part, False), lambda copy: copy.start())
-
-    def loop(low, high, body):
-        def run(m, carry):
-            body(m)
-            return carry
-
-        lax.fori_loop(low, high, run, 0)
-
-    loop(0, LAG, row_step)
-
-    def both(m):
-        row_step(m)
-        column_step(m - LAG)
-
-    loop(LAG, CHUNKS, both)
-    loop(CHUNKS - LAG, CHUNKS, column_step)
-
-    def finish(m):
-        for part in range(2):
-            i = m + part * CHUNKS
-            there = g.at[1 - a, rows(i)]
-            pltpu.make_async_copy(there, there, rcore.at[i]).wait()
-            each(row_copies(m, part), lambda copy: copy.wait_send())
-
-            @pl.when(diagonal)
-            def _():
-                each(column_copies(m, part, True), lambda copy: copy.wait_send())
-
-            @pl.when(~diagonal)
-            def _():
-                each(column_copies(m, part, False), lambda copy: copy.wait_send())
-
-    loop(0, CHUNKS, finish)
+                there = g.at[1 - a, rows(i)]
+                pltpu.make_async_copy(there, there, rcore.at[i]).wait()
+                each(row_copies(m, e, part), lambda copy: copy.wait_send())
+
+                @pl.when(diagonal)
+                def _():
+                    each(column_copies(m, e, part, True), lambda copy: copy.wait_send())
+
+                @pl.when(~diagonal)
+                def _():
+                    each(column_copies(m, e, part, False), lambda copy: copy.wait_send())
+
+        return carry
+
+    lax.fori_loop(0, CHUNKS // 4, finish, 0)
 
 
 def spread(root, half):

time: 818 us -> 332 us (0.41); the launches traced: 808 us -> 332 us
  Pallas kernels: 802 us -> 325 us
    pallas_call x1, Pallas kernels: 610 us -> 133 us  [spread(): pl.pallas_call(functools.partial(spread_kernel, root), out_shape=jax.Shap...]
where the time goes in v2:
time: 332 us
  Pallas kernels  325 us (98%)
  between operations  4.36 us (1%)
    pallas_call x1, Pallas kernels, gather(): pl.pallas_call(gather_kernel, out_shape=(jax.ShapeDtypeStruct((4, 8, FEAT...  144 us
    pallas_call x1, Pallas kernels, spread(): pl.pallas_call(functools.partial(spread_kernel, root), out_shape=jax.Shap...  133 us
    pallas_call x1, Pallas kernels, remaining_matrix(): pl.pallas_call(remaining_kernel, grid_spec=spec, out_shape=(jax.ShapeDtyp...  29.8 us
    pallas_call x1, Pallas kernels, panel_factor(): pl.pallas_call(factor_kernel, grid_spec=spec, out_shape=jax.ShapeDtypeStr...  18.4 us

profile of v2, /device:TPU:40, one launch (start us, length us, event | category | flops | bytes accessed | tf_op | source)
XLA Modules:
  0.0 332.0 jit_solution(14389240505074022916)
XLA Ops:
  1.3 1.3 fusion.1
  5.7 0.6 stack.43.s_ref
  6.3 144.0 %gather.1 = (f32[4,8,440,128]{3,2,1,0:T(8,128)}, f32[16,64,1024]{2,1,0:T(8,128)}, f32[1024,1024]{1,0:T(8,128)}) custom-call(f32[440,128]{1,0:T(8,128)} %x_ref.1, f32[64,1024]{1,0:T(8,128)} %l_ref.1, f32[2048,1024]{1,0:T(8,128)} %d_ref.5), custom_call_target="tpu_custom_call" | custom-call | tf_op jit(solution)/shard_map/gather/pallas_call | solution.py:237
  150.3 18.4 %factor.1 = f32[1024,1024]{1,0:T(8,128)} custom-call(s32[8]{0:T(128)} %stack.43.s_ref, f32[4,8,440,128]{3,2,1,0:T(8,128)} %get-tuple-element.24.xl_ref.xr_ref, f32[4,8,440,128]{3,2,1,0:T(8,128)} %get-tuple-element.24.xl_ref.xr_ref, f32[1024,1024]{1,0:T(8,128)} %bitcast.12, f32[2048,1024]{1,0:T(8,128)} %d_ref.5, f32[1024,1024]{1,0:T(8,128)} %get-tuple-element.26.dx_ref), custom_call_target="tpu_custom_call" | custom-call | tf_op jit(solution)/shard_map/factor/pallas_call | solution.py:333
  168.7 133.5 %conditional.1 = (f32[3,1024,1024]{2,1,0:T(8,128)}) conditional(s32[]{:T(128)} %clamp.3, f32[1024,1024]{1,0:T(8,128)} %factor.1, f32[1024,1024]{1,0:T(8,128)} %factor.1, f32[1024,1024]{1,0:T(8,128)} %factor.1, f32[1024,1024]{1,0:T(8,128)} %factor.1, f32[1024,1024]{1,0:T(8,128)} %factor.1, ...), branch_computations={%region_2.3_spmd, %region_3.4_spmd, %region_4.5_spmd, %region_5.6_... | conditional | bytes 8 | solution.py:543
  168.7 133.3 %spread4.1 = f32[3,1024,1024]{2,1,0:T(8,128)} custom-call(f32[1024,1024]{1,0:T(8,128)} %f_ref.4), custom_call_target="tpu_custom_call" | custom-call | tf_op jit(solution)/shard_map/cond/branch_4_fun/spread4/pallas_call | solution.py:509
  302.2 29.8 %remaining.1 = (f32[2048,1024]{1,0:T(8,128)}, f32[128,1024]{1,0:T(8,128)}) custom-call(s32[8]{0:T(128)} %stack.43.s_ref, f32[4,8,440,128]{3,2,1,0:T(8,128)} %get-tuple-element.24.xl_ref.xr_ref, f32[4,8,440,128]{3,2,1,0:T(8,128)} %get-tuple-element.24.xl_ref.xr_ref, f32[3,1024,1024]{2,1,0:T(8,128)} %get-tuple-element.31.fl_ref.fr_ref.piece_ref, ...), custom_call_target="tpu_custom_call" | custom-call | tf_op jit(solution)/shard_map/remaining/pallas_call | solution.py:379

commit v3 on v2

--- a/solution.py
+++ b/solution.py
@@ -14,8 +14,10 @@
 MESH = pl.DeviceIdType.MESH
 F32 = jnp.float32
 BF16 = jnp.bfloat16
-CHUNKS = 32
-SKEW = 2
+CHUNKS = 64
+SKEW = 4
+PIECES = 5
+CENTER_SKEW = 3
 
 
 def place():
@@ -67,6 +69,13 @@
     return up, down, across
 
 
+def hops(first_ring, d, e, part):
+    rel = (d - e + 4) % 4
+    near_e = e if part == 0 else (4 - e) % 4
+    in_first = d if part == 0 else (4 - d) % 4
+    return jnp.where(first_ring, in_first, near_e + 1 + jnp.minimum(rel, 4 - rel))
+
+
 def column_state(p):
     k = p["xl"] * 4 + p["y"]
     d = (p["z"] - k // 2 + 4) % 4
@@ -90,13 +99,15 @@
 
     started = []
 
-    def send(table, s, way, src=None):
+    def row_copy(table, s, way, src):
         src = at(table, s) if src is None else src
         sems, recv = (sx, rx) if table == 0 else (sl, rl)
         way_index = ("yp", "ym", "xp", "co").index(way)
-        copy = remote(src, at(table, s), sems.at[way_index, s], recv.at[s], near[way])
-        copy.start()
-        started.append(copy)
+        return remote(src, at(table, s), sems.at[way_index, s], recv.at[s], near[way])
+
+    def send(table, s, way, src=None):
+        row_copy(table, s, way, src).start()
+        started.append((table, s, way, src))
 
     def arrived(table, s):
         recv = rx if table == 0 else rl
@@ -115,10 +126,6 @@
         return keep
 
     keep_x = first_sends(0)
-    keep_l = first_sends(1)
-    half = PANEL
-    swap = remote(d_ref.at[pl.ds((1 - a) * half, half)], dx, sd.at[0], sd.at[1], near["co"])
-    swap.start()
 
     def row_steps(table):
         steps = []
@@ -151,49 +158,77 @@
             arrived(0, slot(xs, ys, 1 - a))
     keep_x.wait()
 
-    def column_copies(m, part, src, is_first, dist):
-        up, down, across = branch_flags(is_first, dist, m, part)
-        j = 2 * m + part
-        dst = xg.at[2 + a, j]
-        out = []
-        for index, (flag, way) in enumerate(((up, "zp"), (down, "zm"), (across, "xx"))):
-            out.append((flag, remote(src, dst, sk.at[index, j], rk.at[j], near[way])))
-        return out
-
+    chunks = 4 * PIECES
+    tall = FEAT // PIECES
     true = d >= 0
+
+    def piece(table, n, part):
+        return xg.at[table, 2 * (n // PIECES) + part, pl.ds(pl.multiple_of((n % PIECES) * tall, 8), tall)]
+
+    def column_copies(n, e, part, is_root):
+        c = part * chunks + n
+        src = piece(a, n, part) if is_root else piece(2 + a, n, part)
+        flags = branch_flags(true, 0 * d, e, part) if is_root else branch_flags(first, d, e, part)
+        return [
+            (flag, remote(src, piece(2 + a, n, part), sk.at[index, 2 * e + part], rk.at[c], near[way]))
+            for index, (flag, way) in enumerate(zip(flags, ("zp", "zm", "xx")))
+        ]
+
+    def core_copy(n, part):
+        here = piece(2 + a, n, part)
+        return remote(here, here, sc.at[0], rc.at[0], near["co"])
+
+    def each(copies, act):
+        for flag, copy in copies:
+            @pl.when(flag)
+            def _():
+                act(copy)
 
     @pl.when(diagonal)
     def _():
-        for m in range(4):
+        def issue(group, carry):
+            for e in range(4):
+                for part in range(2):
+                    each(column_copies(4 * group + e, e, part, True), lambda copy: copy.start())
+            return carry
+
+        lax.fori_loop(0, PIECES, issue, 0)
+
+    keep_l = first_sends(1)
+    half = PANEL
+    swap = remote(d_ref.at[pl.ds((1 - a) * half, half)], dx, sd.at[0], sd.at[1], near["co"])
+    swap.start()
+
+    lag = {}
+    for e in range(4):
+        for part in range(2):
+            lag[e, part] = CENTER_SKEW * hops(first, d, e, part)
+
+    rest = row_steps(1)
+    turns = chunks + 6 * CENTER_SKEW
+    cuts = {turns // 5: rest[:3], 2 * turns // 5: rest[3:6], 3 * turns // 5: rest[6:]}
+
+    def turn(t, carry):
+        for cut, steps in cuts.items():
+            @pl.when(t == cut)
+            def _():
+                for run in steps:
+                    run()
+
+        for e in range(4):
             for part in range(2):
-                for flag, copy in column_copies(m, part, xg.at[a, 2 * m + part], true, 0 * d):
-                    @pl.when(flag)
-                    def _():
-                        copy.start()
-
-    def column_step(m):
-        @pl.when(~diagonal)
-        def _():
-            for part in range(2):
-                j = 2 * m + part
-                here = xg.at[2 + a, j]
-                pltpu.make_async_copy(here, here, rk.at[j]).wait()
-                for flag, copy in column_copies(m, part, here, first, d):
-                    @pl.when(flag)
-                    def _():
-                        copy.start()
-                remote(here, here, sc.at[j], rc.at[j], near["co"]).start()
-
-    rest = row_steps(1)
-    for run in rest[:3]:
-        run()
-    column_step(0)
-    for run in rest[3:6]:
-        run()
-    column_step(1)
-    rest[6]()
-    column_step(2)
-    column_step(3)
+                n = t - lag[e, part]
+
+                @pl.when((n >= 0) & (n < chunks) & ((n + 256) % 4 == e) & ~diagonal)
+                def _():
+                    here = piece(2 + a, n, part)
+                    pltpu.make_async_copy(here, here, rk.at[part * chunks + n]).wait()
+                    each(column_copies(n, e, part, False), lambda copy: copy.start())
+                    core_copy(n, part).start()
+
+        return carry
+
+    lax.fori_loop(0, turns, turn, 0)
 
     for xs in range(2):
         for ys in range(4):
@@ -201,31 +236,25 @@
     keep_l.wait()
     swap.wait()
 
-    @pl.when(diagonal)
-    def _():
-        for m in range(4):
-            for part in range(2):
-                for flag, copy in column_copies(m, part, xg.at[a, 2 * m + part], true, 0 * d):
-                    @pl.when(flag)
-                    def _():
-                        copy.wait_send()
+    def whole(ref, sem):
+        pltpu.make_async_copy(ref, ref, sem).wait()
+
+    for e in range(4):
+        for part in range(2):
+            at_root = branch_flags(true, 0 * d, e, part)
+            below = branch_flags(first, d, e, part)
+            for index in range(3):
+                @pl.when((diagonal & at_root[index]) | (~diagonal & below[index]))
+                def _():
+                    whole(xg.at[2 + a, 0], sk.at[index, 2 * e + part])
 
     @pl.when(~diagonal)
     def _():
-        for m in range(4):
-            for part in range(2):
-                j = 2 * m + part
-                here = xg.at[2 + a, j]
-                for flag, copy in column_copies(m, part, here, first, d):
-                    @pl.when(flag)
-                    def _():
-                        copy.wait_send()
-                other = xg.at[3 - a, j]
-                remote(here, here, sc.at[j], rc.at[j], near["co"]).wait_send()
-                pltpu.make_async_copy(other, other, rc.at[j]).wait()
+        whole(xg.at[2 + a], sc.at[0])
+        whole(xg.at[3 - a], rc.at[0])
 
     for copy in started:
-        copy.wait_send()
+        row_copy(*copy).wait_send()
 
 
 def gather(centers, inverse, downdates):
@@ -247,12 +276,12 @@
             dma((2,)),
             dma((16,)),
             dma((16,)),
-            dma((8,)),
-            dma((8,)),
+            dma((8 * PIECES,)),
+            dma((1,)),
             dma((4, 16)),
             dma((4, 16)),
             dma((3, 8)),
-            dma((8,)),
+            dma((1,)),
             dma((2,)),
         ],
         compiler_params=pltpu.CompilerParams(collective_id=0, has_side_effects=True),
@@ -387,13 +416,6 @@
     )(scalars, xg, xg, factors, factors, factors, downdates)
 
 
-def hops(first_ring, d, e, part):
-    rel = (d - e + 4) % 4
-    near_e = e if part == 0 else (4 - e) % 4
-    in_first = d if part == 0 else (4 - d) % 4
-    return jnp.where(first_ring, in_first, near_e + 1 + jnp.minimum(rel, 4 - rel))
-
-
 def spread_kernel(root, f_ref, g, rrow, rcol, rcore, srow, scol, score):
     p = place()
     near = neighbours(p)
@@ -423,10 +445,10 @@
         here = g.at[a, rows(i)]
         flags = branch_flags(first_row, d_row, e, part)
         out = [
-            (flag, remote(here, here, srow.at[n, i], rrow.at[i], near[way]))
+            (flag, remote(here, here, srow.at[n, 2 * e + part], rrow.at[i], near[way]))
             for n, (flag, way) in enumerate(zip(flags, ("yp", "ym", "xp")))
         ]
-        out.append((true, remote(here, here, score.at[i], rcore.at[i], near["co"])))
+        out.append((true, remote(here, here, score.at[0], rcore.at[0], near["co"])))
         return out
 
     def column_copies(m, e, part, from_row):
@@ -435,7 +457,7 @@
         dst = g.at[2, rows(i)]
         flags = branch_flags(true, 0 * d_col, e, part) if from_row else branch_flags(first_col, d_col, e, part)
         return [
-            (flag, remote(src, dst, scol.at[n, i], rcol.at[i], near[way]))
+            (flag, remote(src, dst, scol.at[n, 2 * e + part], rcol.at[i], near[way]))
             for n, (flag, way) in enumerate(zip(flags, ("zp", "zm", "xx")))
         ]
 
@@ -457,7 +479,7 @@
             for part in range(2):
                 m = t - row_lag[e, part]
 
-                @pl.when((m >= 0) & (m < CHUNKS) & ((m + 64) % 4 == e))
+                @pl.when((m >= 0) & (m < CHUNKS) & ((m + 256) % 4 == e))
                 def _():
                     i = m + part * CHUNKS
                     here = g.at[a, rows(i)]
@@ -470,7 +492,7 @@
 
                 n = t - col_lag[e, part]
 
-                @pl.when((n >= 0) & (n < CHUNKS) & ((n + 64) % 4 == e) & ~diagonal)
+                @pl.when((n >= 0) & (n < CHUNKS) & ((n + 256) % 4 == e) & ~diagonal)
                 def _():
                     i = n + part * CHUNKS
                     here = g.at[2, rows(i)]
@@ -481,26 +503,26 @@
 
     lax.fori_loop(0, CHUNKS + 12 * SKEW, turn, 0)
 
-    def finish(group, carry):
-        for e in range(4):
-            m = group * 4 + e
-            for part in range(2):
-                i = m + part * CHUNKS
-                there = g.at[1 - a, rows(i)]
-                pltpu.make_async_copy(there, there, rcore.at[i]).wait()
-                each(row_copies(m, e, part), lambda copy: copy.wait_send())
-
-                @pl.when(diagonal)
+    def whole(ref, sem):
+        pltpu.make_async_copy(ref, ref, sem).wait()
+
+    eighth = PANEL // 8
+    for e in range(4):
+        for part in range(2):
+            along = branch_flags(first_row, d_row, e, part)
+            at_root = branch_flags(true, 0 * d_col, e, part)
+            below = branch_flags(first_col, d_col, e, part)
+            for n in range(3):
+                @pl.when(along[n])
                 def _():
-                    each(column_copies(m, e, part, True), lambda copy: copy.wait_send())
-
-                @pl.when(~diagonal)
+                    whole(g.at[a, pl.ds(0, eighth)], srow.at[n, 2 * e + part])
+
+                @pl.when((diagonal & at_root[n]) | (~diagonal & below[n]))
                 def _():
-                    each(column_copies(m, e, part, False), lambda copy: copy.wait_send())
-
-        return carry
-
-    lax.fori_loop(0, CHUNKS // 4, finish, 0)
+                    whole(g.at[a, pl.ds(0, eighth)], scol.at[n, 2 * e + part])
+
+    whole(g.at[a], score.at[0])
+    whole(g.at[1 - a], rcore.at[0])
 
 
 def spread(root, half):
@@ -511,7 +533,7 @@
         out_shape=jax.ShapeDtypeStruct((3, PANEL, PANEL), F32),
         in_specs=[pl.BlockSpec(memory_space=pltpu.VMEM)],
         out_specs=pl.BlockSpec(memory_space=pl.ANY),
-        scratch_shapes=[dma((n,)), dma((n,)), dma((n,)), dma((3, n)), dma((3, n)), dma((n,))],
+        scratch_shapes=[dma((n,)), dma((n,)), dma((1,)), dma((3, 8)), dma((3, 8)), dma((1,))],
         compiler_params=pltpu.CompilerParams(collective_id=1 + root, has_side_effects=True),
         name="spread" + str(root),
     )(half)

time: 332 us -> 256 us (0.77)
  the two profiles are of different devices: /device:TPU:40 before, /device:TPU:36 now
where the time goes in v3:
time: 256 us; the launch traced here: 255 us
  Pallas kernels  249 us (97%)
  between operations  4.36 us (2%)
    pallas_call x1, Pallas kernels, spread(): pl.pallas_call(functools.partial(spread_kernel, root), out_shape=jax.Shap...  114 us
    pallas_call x1, Pallas kernels, gather(): pl.pallas_call(gather_kernel, out_shape=(jax.ShapeDtypeStruct((4, 8, FEAT...  86.7 us
    pallas_call x1, Pallas kernels, remaining_matrix(): pl.pallas_call(remaining_kernel, grid_spec=spec, out_shape=(jax.ShapeDtyp...  29.8 us
    pallas_call x1, Pallas kernels, panel_factor(): pl.pallas_call(factor_kernel, grid_spec=spec, out_shape=jax.ShapeDtypeStr...  18.4 us

profile of v3, /device:TPU:36, one launch (start us, length us, event | category | flops | bytes accessed | tf_op | source)
XLA Modules:
  0.0 255.4 jit_solution(16234038070834975752)
XLA Ops:
  1.3 1.3 fusion.1
  5.7 0.6 stack.43.s_ref
  6.3 86.7 %gather.1 = (f32[4,8,440,128]{3,2,1,0:T(8,128)}, f32[16,64,1024]{2,1,0:T(8,128)}, f32[1024,1024]{1,0:T(8,128)}) custom-call(f32[440,128]{1,0:T(8,128)} %x_ref.1, f32[64,1024]{1,0:T(8,128)} %l_ref.1, f32[2048,1024]{1,0:T(8,128)} %d_ref.5), custom_call_target="tpu_custom_call" | custom-call | tf_op jit(solution)/shard_map/gather/pallas_call | solution.py:266
  93.0 18.4 %factor.1 = f32[1024,1024]{1,0:T(8,128)} custom-call(s32[8]{0:T(128)} %stack.43.s_ref, f32[4,8,440,128]{3,2,1,0:T(8,128)} %get-tuple-element.24.xl_ref.xr_ref, f32[4,8,440,128]{3,2,1,0:T(8,128)} %get-tuple-element.24.xl_ref.xr_ref, f32[1024,1024]{1,0:T(8,128)} %bitcast.12, f32[2048,1024]{1,0:T(8,128)} %d_ref.5, f32[1024,1024]{1,0:T(8,128)} %get-tuple-element.26.dx_ref), custom_call_target="tpu_custom_call" | custom-call | tf_op jit(solution)/shard_map/factor/pallas_call | solution.py:362
  111.3 114.3 %conditional.1 = (f32[3,1024,1024]{2,1,0:T(8,128)}) conditional(s32[]{:T(128)} %clamp.3, f32[1024,1024]{1,0:T(8,128)} %factor.1, f32[1024,1024]{1,0:T(8,128)} %factor.1, f32[1024,1024]{1,0:T(8,128)} %factor.1, f32[1024,1024]{1,0:T(8,128)} %factor.1, f32[1024,1024]{1,0:T(8,128)} %factor.1, ...), branch_computations={%region_2.3_spmd, %region_3.4_spmd, %region_4.5_spmd, %region_5.6_... | conditional | bytes 8 | solution.py:565
  111.3 114.3 %spread7.1 = f32[3,1024,1024]{2,1,0:T(8,128)} custom-call(f32[1024,1024]{1,0:T(8,128)} %f_ref.7), custom_call_target="tpu_custom_call" | custom-call | tf_op jit(solution)/shard_map/cond/branch_7_fun/spread7/pallas_call | solution.py:531
  225.6 29.8 %remaining.1 = (f32[2048,1024]{1,0:T(8,128)}, f32[128,1024]{1,0:T(8,128)}) custom-call(s32[8]{0:T(128)} %stack.43.s_ref, f32[4,8,440,128]{3,2,1,0:T(8,128)} %get-tuple-element.24.xl_ref.xr_ref, f32[4,8,440,128]{3,2,1,0:T(8,128)} %get-tuple-element.24.xl_ref.xr_ref, f32[3,1024,1024]{2,1,0:T(8,128)} %get-tuple-element.31.fl_ref.fr_ref.piece_ref, ...), custom_call_target="tpu_custom_call" | custom-call | tf_op jit(solution)/shard_map/remaining/pallas_call | solution.py:408

commit v4 on v3

--- a/solution.py
+++ b/solution.py
@@ -15,9 +15,9 @@
 F32 = jnp.float32
 BF16 = jnp.bfloat16
 CHUNKS = 64
-SKEW = 4
+SKEW = 5
 PIECES = 5
-CENTER_SKEW = 3
+CENTER_SKEW = 4
 
 
 def place():
@@ -125,6 +125,9 @@
         keep.start()
         return keep
 
+    half = PANEL
+    swap = remote(d_ref.at[pl.ds((1 - a) * half, half)], dx, sd.at[0], sd.at[1], near["co"])
+    swap.start()
     keep_x = first_sends(0)
 
     def row_steps(table):
@@ -195,9 +198,6 @@
         lax.fori_loop(0, PIECES, issue, 0)
 
     keep_l = first_sends(1)
-    half = PANEL
-    swap = remote(d_ref.at[pl.ds((1 - a) * half, half)], dx, sd.at[0], sd.at[1], near["co"])
-    swap.start()
 
     lag = {}
     for e in range(4):
@@ -331,8 +331,12 @@
         lil[...] = l
 
     raw = gauss_tile(xl_ref, high, low, norm) + jnp.where(s_ref[2] == 1, d_ref[...], dx_ref[...])
-    result = product(split(raw), (lih[...], lil[...]), ((1,), (1,)))
-    out_ref[...] = jnp.where(s_ref[3] == 1, result, 0.0)
+    rh, rl = split(raw)
+    for start in range(0, PANEL, TILE):
+        stop = start + TILE
+        block = (lih[start:stop, :stop], lil[start:stop, :stop])
+        result = product((rh[:, :stop], rl[:, :stop]), block, ((1,), (1,)))
+        out_ref[:, start:stop] = jnp.where(s_ref[3] == 1, result, 0.0)
 
 
 TILE = 256

time: 256 us -> 240 us (0.938)
  the two profiles are of different devices: /device:TPU:36 before, /device:TPU:40 now
where the time goes in v4:
time: 240 us; the launch traced here: 238 us
  Pallas kernels  231 us (96%)
  between operations  4.36 us (2%)
    pallas_call x1, Pallas kernels, spread(): pl.pallas_call(functools.partial(spread_kernel, root), out_shape=jax.Shap...  99.7 us
    pallas_call x1, Pallas kernels, gather(): pl.pallas_call(gather_kernel, out_shape=(jax.ShapeDtypeStruct((4, 8, FEAT...  85.3 us
    pallas_call x1, Pallas kernels, remaining_matrix(): pl.pallas_call(remaining_kernel, grid_spec=spec, out_shape=(jax.ShapeDtyp...  29.8 us
    pallas_call x1, Pallas kernels, panel_factor(): pl.pallas_call(factor_kernel, grid_spec=spec, out_shape=jax.ShapeDtypeStr...  16.6 us

profile of v4, /device:TPU:40, one launch (start us, length us, event | category | flops | bytes accessed | tf_op | source)
XLA Modules:
  0.0 237.8 jit_solution(16591083439289675544)
XLA Ops:
  1.3 1.3 fusion.1
  5.7 0.6 stack.43.s_ref
  6.3 85.3 %gather.1 = (f32[4,8,440,128]{3,2,1,0:T(8,128)}, f32[16,64,1024]{2,1,0:T(8,128)}, f32[1024,1024]{1,0:T(8,128)}) custom-call(f32[440,128]{1,0:T(8,128)} %x_ref.1, f32[64,1024]{1,0:T(8,128)} %l_ref.1, f32[2048,1024]{1,0:T(8,128)} %d_ref.5), custom_call_target="tpu_custom_call" | custom-call | tf_op jit(solution)/shard_map/gather/pallas_call | solution.py:266
  91.6 16.6 %factor.1 = f32[1024,1024]{1,0:T(8,128)} custom-call(s32[8]{0:T(128)} %stack.43.s_ref, f32[4,8,440,128]{3,2,1,0:T(8,128)} %get-tuple-element.24.xl_ref.xr_ref, f32[4,8,440,128]{3,2,1,0:T(8,128)} %get-tuple-element.24.xl_ref.xr_ref, f32[1024,1024]{1,0:T(8,128)} %bitcast.12, f32[2048,1024]{1,0:T(8,128)} %d_ref.5, f32[1024,1024]{1,0:T(8,128)} %get-tuple-element.26.dx_ref), custom_call_target="tpu_custom_call" | custom-call | tf_op jit(solution)/shard_map/factor/pallas_call | solution.py:366
  108.3 99.7 %conditional.1 = (f32[3,1024,1024]{2,1,0:T(8,128)}) conditional(s32[]{:T(128)} %clamp.3, f32[1024,1024]{1,0:T(8,128)} %factor.1, f32[1024,1024]{1,0:T(8,128)} %factor.1, f32[1024,1024]{1,0:T(8,128)} %factor.1, f32[1024,1024]{1,0:T(8,128)} %factor.1, f32[1024,1024]{1,0:T(8,128)} %factor.1, ...), branch_computations={%region_2.3_spmd, %region_3.4_spmd, %region_4.5_spmd, %region_5.6_... | conditional | bytes 8 | solution.py:569
  108.3 99.7 %spread5.1 = f32[3,1024,1024]{2,1,0:T(8,128)} custom-call(f32[1024,1024]{1,0:T(8,128)} %f_ref.5), custom_call_target="tpu_custom_call" | custom-call | tf_op jit(solution)/shard_map/cond/branch_5_fun/spread5/pallas_call | solution.py:535
  208.0 29.8 %remaining.1 = (f32[2048,1024]{1,0:T(8,128)}, f32[128,1024]{1,0:T(8,128)}) custom-call(s32[8]{0:T(128)} %stack.43.s_ref, f32[4,8,440,128]{3,2,1,0:T(8,128)} %get-tuple-element.24.xl_ref.xr_ref, f32[4,8,440,128]{3,2,1,0:T(8,128)} %get-tuple-element.24.xl_ref.xr_ref, f32[3,1024,1024]{2,1,0:T(8,128)} %get-tuple-element.31.fl_ref.fr_ref.piece_ref, ...), custom_call_target="tpu_custom_call" | custom-call | tf_op jit(solution)/shard_map/remaining/pallas_call | solution.py:412
